TPU v7x, 32 devices: a whole 2x2x4 slice. The times are simulated.
32 devices in a mesh: dp: 8 (over y, x, core), tensor: 4 (over z).
Axes of the slice: x: 2, y: 2, z: 4, core: 2. Of those that a mesh axis runs over, the one named last changes fastest.
Arguments:
- hidden_in: bfloat16 [2, 8, 1024, 2048], P(None, None, ('dp', 'tensor')), may hold values from -6 to 6
- lengths: int32 [2, 8], replicated, may hold values from 1 to 1024, 6144 in all within a row
- dealing: int32 [2, 8], replicated, may hold values from 0 to 7, each once within a row
- cotangent: bfloat16 [2, 8, 1024, 2048], P(None, None, ('dp', 'tensor')), may hold values from -6 to 6
- attn_gain: bfloat16 [2048], P(('dp', 'tensor')), may hold values from 0.5 to 1.5
- attn_shift: bfloat16 [2048], P(('dp', 'tensor')), may hold values from -1.5 to 1.5
- ffn_gain: bfloat16 [2048], P(('dp', 'tensor')), may hold values from 0.5 to 1.5
- ffn_shift: bfloat16 [2048], P(('dp', 'tensor')), may hold values from -1.5 to 1.5
- qkv_weight: bfloat16 [2048, 8, 768], P('dp', 'tensor'), may hold values from -0.125 to 0.125
- qkv_bias: bfloat16 [8, 768], P('tensor', 'dp'), may hold values from -0.25 to 0.25
- dense_weight: bfloat16 [8, 256, 2048], P('tensor', 'dp'), may hold values from -1.5 to 1.5
- dense_bias: bfloat16 [2048], P(('dp', 'tensor')), may hold values from -1.5 to 1.5
- fc1_weight: bfloat16 [2048, 8192], P('dp', 'tensor'), may hold values from -0.125 to 0.125
- fc1_bias: bfloat16 [8, 1024], P('tensor', 'dp'), may hold values from -1.5 to 1.5
- fc2_weight: bfloat16 [8192, 2048], P('tensor', 'dp'), may hold values from -0.0625 to 0.0625
- fc2_bias: bfloat16 [2048], P(('dp', 'tensor')), may hold values from -1.5 to 1.5
Outputs:
- output: bfloat16 [2, 8, 1024, 2048], P(None, None, ('dp', 'tensor'))
- input_grad: bfloat16 [2, 8, 1024, 2048], P(None, None, ('dp', 'tensor'))
- attngain_grad: float32 [2048], P(('dp', 'tensor'))
- attnshift_grad: float32 [2048], P(('dp', 'tensor'))
- ffngain_grad: float32 [2048], P(('dp', 'tensor'))
- ffnshift_grad: float32 [2048], P(('dp', 'tensor'))
- qkvweight_grad: float32 [2048, 8, 768], P('dp', 'tensor')
- qkvbias_grad: float32 [8, 768], P('tensor', 'dp')
- denseweight_grad: float32 [8, 256, 2048], P('tensor', 'dp')
- densebias_grad: float32 [2048], P(('dp', 'tensor'))
- fc1weight_grad: float32 [2048, 8192], P('dp', 'tensor')
- fc1bias_grad: float32 [8, 1024], P('tensor', 'dp')
- fc2weight_grad: float32 [8192, 2048], P('tensor', 'dp')
- fc2bias_grad: float32 [2048], P(('dp', 'tensor'))
Inputs may be any that keep to these rules, and one draw needn't show every extreme that they name: lengths[m, j] belongs to the sequence in input slot dealing[m, j]; in each micro-batch the lengths sum to 6144 and the longest is 1024. Each row of dealing holds every slot number once.
All inputs are finite; a program needn't handle non-finite values.
Results may differ from a plain program's by a relative error of at most 0.013.
Values may be sent and summed in bfloat16 or wider, within the bound.
No kernel may reach another device: no remote copies, remote signals or barrier semaphores. Data moves between devices by JAX's collectives and lax.ppermute only.
A program may use at most 320 MiB of HBM per device.

v0:
```python
import math
import jax
import jax.numpy as jnp
from jax import lax
from jax.sharding import PartitionSpec as P

HD = 256
ROT = 64
EPSILON = 1e-05
ROPE_BASE = 10000.0
NEG_FILL = -1e30
SQRT_HALF = 0.7071067811865476
INV_ROOT_TWO_PI = 0.3989422804014327


def normalize(residual, gain, shift):
    centred = residual - jnp.mean(residual, axis=-1, keepdims=True)
    scaling = lax.rsqrt(jnp.mean(centred * centred, axis=-1, keepdims=True) + EPSILON)
    unit_rows = centred * scaling
    return (unit_rows * gain + shift, unit_rows, scaling)


def norm_back(grad_out, unit_rows, scaling, gain):
    grad_unit = grad_out * gain
    return scaling * (
        grad_unit
        - jnp.mean(grad_unit, axis=-1, keepdims=True)
        - unit_rows * jnp.mean(grad_unit * unit_rows, axis=-1, keepdims=True)
    )


def angles(positions):
    freqs = jnp.exp(jnp.arange(ROT // 2, dtype=jnp.float32) * (-2.0 * math.log(ROPE_BASE) / ROT))
    phases = positions.astype(jnp.float32)[:, None] * freqs[None, :]
    return (jnp.cos(phases), jnp.sin(phases))


def rotate(heads, cosines, sines):
    half_rot = ROT // 2
    lead_part = heads[..., :half_rot]
    trail_part = heads[..., half_rot:ROT]
    cos_rows = cosines[:, None, :]
    sin_rows = sines[:, None, :]
    return jnp.concatenate(
        [
            lead_part * cos_rows - trail_part * sin_rows,
            trail_part * cos_rows + lead_part * sin_rows,
            heads[..., ROT:],
        ],
        axis=-1,
    )


def take_slots(table, order):
    return jnp.take(table, order, axis=0)


def per_device(
    hidden_in,
    lengths,
    dealing,
    cotangent,
    attn_gain,
    attn_shift,
    ffn_gain,
    ffn_shift,
    qkv_weight,
    qkv_bias,
    dense_weight,
    dense_bias,
    fc1_weight,
    fc1_bias,
    fc2_weight,
    fc2_bias,
):
    n_tensor = lax.axis_size("tensor")
    n_data = lax.axis_size("dp")
    group_index = lax.axis_index("dp")
    micro_count, seq_count, piece_rows, width = hidden_in.shape
    local_rows = n_data * piece_rows
    seq_rows = n_tensor * local_rows
    block_rows = min(512, seq_rows)
    block_count = seq_rows // block_rows
    scale = 1.0 / math.sqrt(HD)
    sent_in = jax.vmap(take_slots)(hidden_in, dealing)
    sent_grad = jax.vmap(take_slots)(cotangent, dealing)
    got_in, got_grad = (
        lax.all_to_all(sent_in, "dp", split_axis=1, concat_axis=2, tiled=True),
        lax.all_to_all(sent_grad, "dp", split_axis=1, concat_axis=2, tiled=True),
    )
    small = (
        lax.all_gather(attn_gain, ("dp", "tensor"), axis=0, tiled=True),
        lax.all_gather(attn_shift, ("dp", "tensor"), axis=0, tiled=True),
        lax.all_gather(ffn_gain, ("dp", "tensor"), axis=0, tiled=True),
        lax.all_gather(ffn_shift, ("dp", "tensor"), axis=0, tiled=True),
        lax.all_gather(dense_bias, ("dp", "tensor"), axis=0, tiled=True),
        lax.all_gather(fc2_bias, ("dp", "tensor"), axis=0, tiled=True),
    )
    gain_one, shift_one, gain_two, shift_two, dense_shift, fc2_shift = [
        piece.astype(jnp.float32) for piece in small
    ]
    shard_set = (qkv_weight, qkv_bias, dense_weight, fc1_weight, fc1_bias, fc2_weight)

    def current_set():
        return (
            lax.all_gather(shard_set[0], "dp", axis=0, tiled=True),
            lax.all_gather(shard_set[1], "dp", axis=1, tiled=True),
            lax.all_gather(shard_set[2], "dp", axis=1, tiled=True),
            lax.all_gather(shard_set[3], "dp", axis=0, tiled=True),
            lax.all_gather(shard_set[4], "dp", axis=1, tiled=True),
            lax.all_gather(shard_set[5], "dp", axis=1, tiled=True),
        )

    row_ids = jnp.arange(seq_rows, dtype=jnp.int32)
    part_ids = row_ids // local_rows
    within = row_ids % local_rows
    positions = (within // piece_rows * n_tensor + part_ids) * piece_rows + within % piece_rows
    cosines, sines = angles(positions)
    my_lengths = lax.dynamic_index_in_dim(lengths, group_index, axis=1, keepdims=False)
    starts = jnp.arange(block_count, dtype=jnp.int32) * block_rows
    heads_here = qkv_weight.shape[1]
    units_here = fc1_weight.shape[1]
    weight_zero = (
        jnp.zeros((width, heads_here, 3 * HD), jnp.float32),
        jnp.zeros((heads_here, 3 * HD), jnp.float32),
        jnp.zeros((heads_here, HD, width), jnp.float32),
        jnp.zeros((width, units_here), jnp.float32),
        jnp.zeros((heads_here, units_here // heads_here), jnp.float32),
        jnp.zeros((units_here, width), jnp.float32),
    )
    small_zero = tuple((jnp.zeros((width,), jnp.float32) for index_slot in range(6)))

    def micro_step(totals, item):
        weight_totals, small_totals = totals
        rows_in, rows_grad, seq_length = item
        qkv_full, qkv_shift, dense_full, fc1_full, fc1_shift, fc2_full = current_set()
        residual = rows_in.astype(jnp.float32)
        normed_one, unit_one, scale_one = normalize(residual, gain_one, shift_one)
        normed_two = unit_one * gain_two + shift_two
        full_one, full_two = (
            lax.all_gather(normed_one.astype(jnp.bfloat16), "tensor", axis=0, tiled=True),
            lax.all_gather(normed_two.astype(jnp.bfloat16), "tensor", axis=0, tiled=True),
        )
        projected = jnp.einsum(
            "ld,dhe->lhe", full_one, qkv_full, preferred_element_type=jnp.float32
        ) + qkv_shift.astype(jnp.float32)
        queries = rotate(projected[..., :HD], cosines, sines).astype(jnp.bfloat16)
        key_rows = rotate(projected[..., HD : 2 * HD], cosines, sines).astype(jnp.bfloat16)
        value_rows = projected[..., 2 * HD :].astype(jnp.bfloat16)

        def mask_for(row_start):
            q_pos = lax.dynamic_slice_in_dim(positions, row_start, block_rows, 0)
            return (positions[None, :] <= q_pos[:, None]) & (positions[None, :] < seq_length)

        def attend(row_start):
            q_block = lax.dynamic_slice_in_dim(queries, row_start, block_rows, 0)
            scores = (
                jnp.einsum("qhe,khe->hqk", q_block, key_rows, preferred_element_type=jnp.float32)
                * scale
            )
            scores = jnp.where(mask_for(row_start)[None], scores, NEG_FILL)
            row_max = jnp.max(scores, axis=-1, keepdims=True)
            expo = jnp.exp(scores - row_max)
            row_sum = jnp.sum(expo, axis=-1, keepdims=True)
            softmax_w = (expo / row_sum).astype(jnp.bfloat16)
            mixed_block = jnp.einsum(
                "hqk,khe->qhe", softmax_w, value_rows, preferred_element_type=jnp.float32
            ).astype(jnp.bfloat16)
            return (mixed_block, (row_max + jnp.log(row_sum))[..., 0])

        mixed_blocks, lse_blocks = lax.map(attend, starts)
        mixed = mixed_blocks.reshape(seq_rows, heads_here, HD)
        attn_part = jnp.einsum("lhe,hed->ld", mixed, dense_full, preferred_element_type=jnp.float32)
        preact = jnp.dot(
            full_two, fc1_full, preferred_element_type=jnp.float32
        ) + fc1_shift.reshape(-1).astype(jnp.float32)
        activation = jax.nn.gelu(preact, approximate=False).astype(jnp.bfloat16)
        ffn_part = jnp.dot(activation, fc2_full, preferred_element_type=jnp.float32)
        branch = lax.psum_scatter(attn_part + ffn_part, "tensor", scatter_dimension=0, tiled=True)
        output_rows = (residual + branch + dense_shift + fc2_shift).astype(jnp.bfloat16)
        back_set = current_set()
        grad_full = lax.all_gather(rows_grad, "tensor", axis=0, tiled=True)
        grad_dense = jnp.einsum("lhe,ld->hed", mixed, grad_full, preferred_element_type=jnp.float32)
        grad_mixed = jnp.einsum(
            "ld,hed->lhe", grad_full, back_set[2], preferred_element_type=jnp.float32
        ).astype(jnp.bfloat16)
        grad_fc2 = jnp.einsum(
            "lf,ld->fd", activation, grad_full, preferred_element_type=jnp.float32
        )
        grad_act = jnp.einsum(
            "ld,fd->lf", grad_full, back_set[5], preferred_element_type=jnp.float32
        )
        normal_cdf = 0.5 * (1.0 + lax.erf(preact * SQRT_HALF))
        slope = normal_cdf + preact * jnp.exp(-0.5 * preact * preact) * INV_ROOT_TWO_PI
        grad_pre = (grad_act * slope).astype(jnp.bfloat16)
        grad_fc1 = jnp.einsum("ld,lf->df", full_two, grad_pre, preferred_element_type=jnp.float32)
        grad_fc1b = jnp.sum(grad_pre.astype(jnp.float32), axis=0).reshape(
            heads_here, units_here // heads_here
        )
        grad_second = jnp.einsum(
            "lf,df->ld", grad_pre, back_set[3], preferred_element_type=jnp.float32
        )

        def back_block(carry, block_item):
            key_grad, value_grad = carry
            row_start, lse_block = block_item
            q_block = lax.dynamic_slice_in_dim(queries, row_start, block_rows, 0)
            grad_block = lax.dynamic_slice_in_dim(grad_mixed, row_start, block_rows, 0)
            scores = (
                jnp.einsum("qhe,khe->hqk", q_block, key_rows, preferred_element_type=jnp.float32)
                * scale
            )
            scores = jnp.where(mask_for(row_start)[None], scores, NEG_FILL)
            softmax_f = jnp.exp(scores - lse_block[..., None])
            softmax_w = softmax_f.astype(jnp.bfloat16)
            value_grad = value_grad + jnp.einsum(
                "hqk,qhe->khe", softmax_w, grad_block, preferred_element_type=jnp.float32
            )
            grad_soft = jnp.einsum(
                "qhe,khe->hqk", grad_block, value_rows, preferred_element_type=jnp.float32
            )
            grad_scores = (
                softmax_f * (grad_soft - jnp.sum(softmax_f * grad_soft, axis=-1, keepdims=True))
            ).astype(jnp.bfloat16)
            query_part = (
                jnp.einsum(
                    "hqk,khe->qhe", grad_scores, key_rows, preferred_element_type=jnp.float32
                )
                * scale
            )
            key_grad = (
                key_grad
                + jnp.einsum(
                    "hqk,qhe->khe", grad_scores, q_block, preferred_element_type=jnp.float32
                )
                * scale
            )
            return ((key_grad, value_grad), query_part)

        zero_heads = jnp.zeros((seq_rows, heads_here, HD), jnp.float32)
        (key_grad, value_grad), query_parts = lax.scan(
            back_block, (zero_heads, zero_heads), (starts, lse_blocks)
        )
        query_grad = query_parts.reshape(seq_rows, heads_here, HD)
        grad_qkv = jnp.concatenate(
            [rotate(query_grad, cosines, -sines), rotate(key_grad, cosines, -sines), value_grad],
            axis=-1,
        ).astype(jnp.bfloat16)
        grad_qkvw = jnp.einsum(
            "ld,lhe->dhe", full_one, grad_qkv, preferred_element_type=jnp.float32
        )
        grad_qkvb = jnp.sum(grad_qkv.astype(jnp.float32), axis=0)
        grad_first = jnp.einsum(
            "lhe,dhe->ld", grad_qkv, back_set[0], preferred_element_type=jnp.float32
        )
        upstream = rows_grad.astype(jnp.float32)
        upstream_sum = jnp.sum(upstream, axis=0)
        norm_one, norm_two = (
            lax.psum_scatter(grad_first, "tensor", scatter_dimension=0, tiled=True),
            lax.psum_scatter(grad_second, "tensor", scatter_dimension=0, tiled=True),
        )
        input_rows = (
            upstream
            + norm_back(norm_one, unit_one, scale_one, gain_one)
            + norm_back(norm_two, unit_one, scale_one, gain_two)
        ).astype(jnp.bfloat16)
        small_terms = (
            jnp.sum(norm_one * unit_one, axis=0),
            jnp.sum(norm_one, axis=0),
            jnp.sum(norm_two * unit_one, axis=0),
            jnp.sum(norm_two, axis=0),
            upstream_sum,
            upstream_sum,
        )
        weight_terms = (grad_qkvw, grad_qkvb, grad_dense, grad_fc1, grad_fc1b, grad_fc2)
        new_weights = tuple((total + term for total, term in zip(weight_totals, weight_terms)))
        new_small = tuple((total + term for total, term in zip(small_totals, small_terms)))
        return ((new_weights, new_small), (output_rows, input_rows))

    (weight_totals, small_totals), (output_rows, input_rows) = lax.scan(
        micro_step, (weight_zero, small_zero), (got_in[:, 0], got_grad[:, 0], my_lengths)
    )
    weight_sums = (
        lax.psum_scatter(
            weight_totals[0].astype(jnp.bfloat16), "dp", scatter_dimension=0, tiled=True
        ).astype(jnp.float32),
        lax.psum_scatter(
            weight_totals[1].astype(jnp.bfloat16), "dp", scatter_dimension=1, tiled=True
        ).astype(jnp.float32),
        lax.psum_scatter(
            weight_totals[2].astype(jnp.bfloat16), "dp", scatter_dimension=1, tiled=True
        ).astype(jnp.float32),
        lax.psum_scatter(
            weight_totals[3].astype(jnp.bfloat16), "dp", scatter_dimension=0, tiled=True
        ).astype(jnp.float32),
        lax.psum_scatter(
            weight_totals[4].astype(jnp.bfloat16), "dp", scatter_dimension=1, tiled=True
        ).astype(jnp.float32),
        lax.psum_scatter(
            weight_totals[5].astype(jnp.bfloat16), "dp", scatter_dimension=1, tiled=True
        ).astype(jnp.float32),
    )
    small_sums = lax.psum_scatter(small_totals, ("dp", "tensor"), scatter_dimension=0, tiled=True)
    back_out, back_grad = (
        lax.all_to_all(output_rows[:, None], "dp", split_axis=2, concat_axis=1, tiled=True),
        lax.all_to_all(input_rows[:, None], "dp", split_axis=2, concat_axis=1, tiled=True),
    )
    slot_ids = jnp.arange(seq_count, dtype=jnp.int32)
    inverse = jnp.sum(
        jnp.where(dealing[:, :, None] == slot_ids[None, None, :], slot_ids[None, :, None], 0),
        axis=1,
    )
    output = jax.vmap(take_slots)(back_out, inverse)
    input_grad = jax.vmap(take_slots)(back_grad, inverse)
    return (
        output,
        input_grad,
        small_sums[0],
        small_sums[1],
        small_sums[2],
        small_sums[3],
        weight_sums[0],
        weight_sums[1],
        weight_sums[2],
        small_sums[4],
        weight_sums[3],
        weight_sums[4],
        weight_sums[5],
        small_sums[5],
    )


def solution(mesh):
    return jax.shard_map(
        per_device,
        mesh=mesh,
        in_specs=(
            P(None, None, ("dp", "tensor"), None),
            P(),
            P(),
            P(None, None, ("dp", "tensor"), None),
            P(("dp", "tensor")),
            P(("dp", "tensor")),
            P(("dp", "tensor")),
            P(("dp", "tensor")),
            P("dp", "tensor", None),
            P("tensor", "dp"),
            P("tensor", "dp", None),
            P(("dp", "tensor")),
            P("dp", "tensor"),
            P("tensor", "dp"),
            P("tensor", "dp"),
            P(("dp", "tensor")),
        ),
        out_specs=(
            P(None, None, ("dp", "tensor"), None),
            P(None, None, ("dp", "tensor"), None),
            P(("dp", "tensor")),
            P(("dp", "tensor")),
            P(("dp", "tensor")),
            P(("dp", "tensor")),
            P("dp", "tensor", None),
            P("tensor", "dp"),
            P("tensor", "dp", None),
            P(("dp", "tensor")),
            P("dp", "tensor"),
            P("tensor", "dp"),
            P("tensor", "dp"),
            P(("dp", "tensor")),
        ),
        check_vma=False,
    )
```

profile of v0, /device:TPU:0, one launch (start us, length us, event | category | flops | bytes accessed | tf_op | source)
XLA Modules:
  0.0 2300.3 jit_solution(938326112984021490)
XLA Ops:
  28.8 23.3 %all-to-all-done = bf16[2,8,32,2048]{3,2,0,1:T(8,128)(2,1)S(1)} async-done(((bf16[2,8,32,2048]{3,2,0,1:T(8,128)(2,1)}), bf16[2,8,32,2048]{3,2,0,1:T(8,128)(2,1)S(1)}, u32[]{:S(2)}, u32[]{:S(2)}) %all-to-all-start) | async-done | bytes 2097184 | tf_op jit(solution)/shard_map/all_to_all | solution.py:88
  58.2 58.6 %all-reduce.14 = (bf16[2048]{0:T(1024)(128)(2,1)S(1)}, bf16[2048]{0:T(1024)(128)(2,1)S(1)}, bf16[2048]{0:T(1024)(128)(2,1)S(1)}, bf16[2048]{0:T(1024)(128)(2,1)S...) all-reduce(bf16[2048]{0:T(1024)(128)(2,1)S(1)} %dynamic-update-slic, ...), channel_id=1, replica_groups=mesh['dp'=8,'tensor'=4] {'dp','tensor'}, use_global_device_ids=true, to_apply=%add | all-reduce | flops 12288 | bytes 49152
  127.4 1772.7 %while.89 = (s32[]{:T(128)}, f32[2048,2,768]{2,0,1:T(8,128)}, f32[2,768]{1,0:T(2,128)}, f32[2,256,2048]{2,1,0:T(8,128)}, f32[2048,2048]{1,0:T(8,128)}, /*index=5...) while((s32[]{:T(128)}, f32[2048,2,768]{2,0,1:T(8,128)}, ...), condition=%wide.region_24.26_spmd.clone.clone.clone.clone, body=%wide.region_0.25_spmd.clone.clone.clone.clone.sunk | while | flops 81338195968 | bytes 859343296 | solution.py:280
  157.5 82.4 %all-gather.26.cloned.1.call-done = bf16[1,1024,2048]{2,1,0:T(8,128)(2,1)} async-done(((bf16[1,256,2048]{2,1,0:T(8,128)(2,1)}), bf16[1,1024,2048]{2,1,0:T(8,128)(2,1)}) %all-gather.26.cloned.1.call-update) | async-done | bytes 4194320 | tf_op jit(solution)/shard_map/while/body/eval_jaxpr/all_gather | solution.py:182
  246.1 74.7 %all-gather.22.cloned.1.call-done = bf16[1024,2048]{1,0:T(8,128)(2,1)} async-done(((bf16[256,2048]{1,0:T(8,128)(2,1)}), bf16[1024,2048]{1,0:T(8,128)(2,1)}) %all-gather.22.cloned.1.call-update) | async-done | bytes 4194320 | tf_op jit(solution)/shard_map/while/body/eval_jaxpr/all_gather | solution.py:141
  320.8 47.0 %all-gather.20.cloned.1.call-done = bf16[2048,2,768]{0,2,1:T(8,128)(2,1)} async-done(((bf16[256,2,768]{0,2,1:T(8,128)(2,1)}), bf16[2048,2,768]{0,2,1:T(8,128)(2,1)}) %all-gather.20.cloned.1.call-update) | async-done | bytes 6291472 | tf_op jit(solution)/shard_map/while/body/eval_jaxpr/all_gather | solution.py:106
  405.0 87.3 %while.91 = (s32[]{:T(128)}, f32[1024,2,256]{0,2,1:T(8,128)}, f32[1024,2,256]{0,2,1:T(8,128)}, f32[2,512,2,256]{1,0,3,2:T(2,128)}, s32[2]{0:T(128)S(1)}, /*index...) while((s32[]{:T(128)}, f32[1024,2,256]{0,2,1:T(8,128)}, ...), condition=%wide.region_9.10_spmd.clone.clone, body=%wide.region_7.9_spmd.clone.clone.sunk | while | flops 2704015360 | bytes 111194568 | solution.py:241
  538.0 31.3 %fusion.250 = (bf16[1024,2048]{1,0:T(8,128)(2,1)}, f32[1024,2048]{1,0:T(8,128)}) fusion(f32[2048]{0:T(1024)S(1)} %bitcast.334, bf16[1024,2048]{1,0:T(8,128)(2,1)} %all-gather.28.cloned.1.call-done, bf16[2048,2048]{1,0:T(8,128)(2,1)} %all-gather.30.cloned.1.call-done), kind=kOutput, calls=%fused_computation.67.clone.1 | convolution fusion | flops 8728346624 | bytes 25174016 | tf_op jit(solution)/shard_map/while/body/eval_jaxpr/dot_general | solution.py:174
  665.1 44.9 %reduce-scatter.25.cloned.1.call-done = f32[256,2048]{1,0:T(8,128)} async-done(((f32[1024,2048]{1,0:T(8,128)}), f32[256,2048]{1,0:T(8,128)}) %reduce-scatter.25.cloned.1.call-update) | async-done | bytes 2097168 | tf_op jit(solution)/shard_map/while/body/eval_jaxpr/reduce_scatter | solution.py:259
  710.0 147.6 %reduce-scatter.23.cloned.1.call-done = f32[256,2048]{1,0:T(8,128)} async-done(((f32[1024,2048]{1,0:T(8,128)}), f32[256,2048]{1,0:T(8,128)}) %reduce-scatter.23.cloned.1.call-update) | async-done | bytes 2097168 | tf_op jit(solution)/shard_map/while/body/eval_jaxpr/reduce_scatter | solution.py:260
  861.8 143.2 %reduce-scatter.27.cloned.1.call-done = f32[256,2048]{1,0:T(8,128)} async-done(((f32[1024,2048]{1,0:T(8,128)}), f32[256,2048]{1,0:T(8,128)}) %reduce-scatter.27.cloned.1.call-update) | async-done | bytes 2097168 | tf_op jit(solution)/shard_map/while/body/eval_jaxpr/reduce_scatter | solution.py:179
  1041.8 82.2 %all-gather.26.cloned.1.call-done = bf16[1,1024,2048]{2,1,0:T(8,128)(2,1)} async-done(((bf16[1,256,2048]{2,1,0:T(8,128)(2,1)}), bf16[1,1024,2048]{2,1,0:T(8,128)(2,1)}) %all-gather.26.cloned.1.call-update) | async-done | bytes 4194320 | tf_op jit(solution)/shard_map/while/body/eval_jaxpr/all_gather | solution.py:182
  1130.2 74.7 %all-gather.22.cloned.1.call-done = bf16[1024,2048]{1,0:T(8,128)(2,1)} async-done(((bf16[256,2048]{1,0:T(8,128)(2,1)}), bf16[1024,2048]{1,0:T(8,128)(2,1)}) %all-gather.22.cloned.1.call-update) | async-done | bytes 4194320 | tf_op jit(solution)/shard_map/while/body/eval_jaxpr/all_gather | solution.py:141
  1204.9 47.0 %all-gather.20.cloned.1.call-done = bf16[2048,2,768]{0,2,1:T(8,128)(2,1)} async-done(((bf16[256,2,768]{0,2,1:T(8,128)(2,1)}), bf16[2048,2,768]{0,2,1:T(8,128)(2,1)}) %all-gather.20.cloned.1.call-update) | async-done | bytes 6291472 | tf_op jit(solution)/shard_map/while/body/eval_jaxpr/all_gather | solution.py:106
  1289.2 87.3 %while.91 = (s32[]{:T(128)}, f32[1024,2,256]{0,2,1:T(8,128)}, f32[1024,2,256]{0,2,1:T(8,128)}, f32[2,512,2,256]{1,0,3,2:T(2,128)}, s32[2]{0:T(128)S(1)}, /*index...) while((s32[]{:T(128)}, f32[1024,2,256]{0,2,1:T(8,128)}, ...), condition=%wide.region_9.10_spmd.clone.clone, body=%wide.region_7.9_spmd.clone.clone.sunk | while | flops 2704015360 | bytes 111194568 | solution.py:241
  1422.2 31.4 %fusion.250 = (bf16[1024,2048]{1,0:T(8,128)(2,1)}, f32[1024,2048]{1,0:T(8,128)}) fusion(f32[2048]{0:T(1024)S(1)} %bitcast.334, bf16[1024,2048]{1,0:T(8,128)(2,1)} %all-gather.28.cloned.1.call-done, bf16[2048,2048]{1,0:T(8,128)(2,1)} %all-gather.30.cloned.1.call-done), kind=kOutput, calls=%fused_computation.67.clone.1 | convolution fusion | flops 8728346624 | bytes 25174016 | tf_op jit(solution)/shard_map/while/body/eval_jaxpr/dot_general | solution.py:174
  1559.4 34.4 %reduce-scatter.25.cloned.1.call-done = f32[256,2048]{1,0:T(8,128)} async-done(((f32[1024,2048]{1,0:T(8,128)}), f32[256,2048]{1,0:T(8,128)}) %reduce-scatter.25.cloned.1.call-update) | async-done | bytes 2097168 | tf_op jit(solution)/shard_map/while/body/eval_jaxpr/reduce_scatter | solution.py:259
  1593.8 147.6 %reduce-scatter.23.cloned.1.call-done = f32[256,2048]{1,0:T(8,128)} async-done(((f32[1024,2048]{1,0:T(8,128)}), f32[256,2048]{1,0:T(8,128)}) %reduce-scatter.23.cloned.1.call-update) | async-done | bytes 2097168 | tf_op jit(solution)/shard_map/while/body/eval_jaxpr/reduce_scatter | solution.py:260
  1745.6 143.2 %reduce-scatter.27.cloned.1.call-done = f32[256,2048]{1,0:T(8,128)} async-done(((f32[1024,2048]{1,0:T(8,128)}), f32[256,2048]{1,0:T(8,128)}) %reduce-scatter.27.cloned.1.call-update) | async-done | bytes 2097168 | tf_op jit(solution)/shard_map/while/body/eval_jaxpr/reduce_scatter | solution.py:179
  1961.7 22.5 all-to-all-done.3
  1990.1 64.1 %all-reduce.13 = (f32[2048]{0:T(1024)S(1)}, f32[2048]{0:T(1024)S(1)}, f32[2048]{0:T(1024)S(1)}, f32[2048]{0:T(1024)S(1)}, f32[2048]{0:T(1024)S(1)}, /*index=5*/f32[2048]{0:T(1024)S(1)}) all-reduce(f32[2048]{0:T(1024)S(1)} %copy-done.33, f32[2048]{0:T(1024)S(1)} %copy-done.36, ...), channel_id=6, replica_groups=mesh['dp'=8,'tensor'=4] {'dp','tensor'}, use_global_device_ids=true, to_apply=%region_26.28.clone | all-reduce | flops 12288 | bytes 98304
  2077.5 62.7 %all-reduce.17.cloned.1.call-done = bf16[2048,2,768]{2,1,0:T(2,128)(2,1)} async-done(((bf16[2048,2,768]{2,1,0:T(2,128)(2,1)}), bf16[2048,2,768]{2,1,0:T(2,128)(2,1)}) %all-reduce.17.cloned.1.call-update) | async-done | bytes 6291472
  2143.0 72.0 %reduce-scatter.15.cloned.1.call-done = bf16[256,2048]{1,0:T(8,128)(2,1)} async-done(((bf16[2048,2048]{1,0:T(8,128)(2,1)}), bf16[256,2048]{1,0:T(8,128)(2,1)}) %reduce-scatter.15.cloned.1.call-update) | async-done | bytes 1048592 | tf_op jit(solution)/shard_map/reduce_scatter | solution.py:293
  2217.7 72.2 %reduce-scatter.17.cloned.1.call-done = bf16[2048,256]{1,0:T(8,128)(2,1)} async-done(((bf16[2048,2048]{1,0:T(8,128)(2,1)}), bf16[2048,256]{1,0:T(8,128)(2,1)}) %reduce-scatter.17.cloned.1.call-update) | async-done | bytes 1048592 | tf_op jit(solution)/shard_map/reduce_scatter | solution.py:299
  (643 shorter events, 786.0 us)
Async XLA Ops:
  128.5 111.3 %all-gather.26.cloned.1.call-start = ((), (), s32[]{:S(2)}) async-start(), calls=%async_computation.21 | async-start | bytes 5242880 | tf_op jit(solution)/shard_map/while/body/eval_jaxpr/all_gather | solution.py:182
  131.7 189.1 %all-gather.22.cloned.1.call-start = ((), (), s32[]{:S(2)}) async-start(), calls=%async_computation.19 | async-start | bytes 5242880 | tf_op jit(solution)/shard_map/while/body/eval_jaxpr/all_gather | solution.py:141
  135.4 232.4 %all-gather.20.cloned.1.call-start = ((), (), s32[]{:S(2)}) async-start(), calls=%async_computation.18 | async-start | bytes 7077888 | tf_op jit(solution)/shard_map/while/body/eval_jaxpr/all_gather | solution.py:106
  135.9 402.0 %all-gather.28.cloned.1.call-start = ((), (), s32[]{:S(2)}) async-start(), calls=%async_computation.22 | async-start | bytes 5242880 | tf_op jit(solution)/shard_map/while/body/eval_jaxpr/all_gather | solution.py:142
  136.5 401.5 %all-gather.30.cloned.1.call-start = ((), (), s32[]{:S(2)}) async-start(), calls=%async_computation.23 | async-start | bytes 9437184 | tf_op jit(solution)/shard_map/while/body/eval_jaxpr/all_gather | solution.py:109
  137.1 432.2 %all-gather.32.cloned.1.call-start = ((), (), s32[]{:S(2)}) async-start(), calls=%async_computation.24 | async-start | bytes 9437184 | tf_op jit(solution)/shard_map/while/body/eval_jaxpr/all_gather | solution.py:111
  137.9 572.1 %reduce-scatter.25.cloned.1.call-start = ((), (), s32[]{:S(2)}) async-start(), calls=%async_computation.26 | async-start | bytes 10485760 | tf_op jit(solution)/shard_map/while/body/eval_jaxpr/reduce_scatter | solution.py:259
  528.6 329.0 %reduce-scatter.23.cloned.1.call-start = ((), (), s32[]{:S(2)}) async-start(), calls=%async_computation.25 | async-start | bytes 10485760 | tf_op jit(solution)/shard_map/while/body/eval_jaxpr/reduce_scatter | solution.py:260
  599.9 405.1 %reduce-scatter.27.cloned.1.call-start = ((), (), s32[]{:S(2)}) async-start(), calls=%async_computation.27 | async-start | bytes 10485760 | tf_op jit(solution)/shard_map/while/body/eval_jaxpr/reduce_scatter | solution.py:179
  1011.1 112.9 %all-gather.26.cloned.1.call-start = ((), (), s32[]{:S(2)}) async-start(), calls=%async_computation.21 | async-start | bytes 5242880 | tf_op jit(solution)/shard_map/while/body/eval_jaxpr/all_gather | solution.py:182
  1014.3 190.6 %all-gather.22.cloned.1.call-start = ((), (), s32[]{:S(2)}) async-start(), calls=%async_computation.19 | async-start | bytes 5242880 | tf_op jit(solution)/shard_map/while/body/eval_jaxpr/all_gather | solution.py:141
  1018.0 233.9 %all-gather.20.cloned.1.call-start = ((), (), s32[]{:S(2)}) async-start(), calls=%async_computation.18 | async-start | bytes 7077888 | tf_op jit(solution)/shard_map/while/body/eval_jaxpr/all_gather | solution.py:106
  1018.5 403.6 %all-gather.28.cloned.1.call-start = ((), (), s32[]{:S(2)}) async-start(), calls=%async_computation.22 | async-start | bytes 5242880 | tf_op jit(solution)/shard_map/while/body/eval_jaxpr/all_gather | solution.py:142
  1019.1 403.0 %all-gather.30.cloned.1.call-start = ((), (), s32[]{:S(2)}) async-start(), calls=%async_computation.23 | async-start | bytes 9437184 | tf_op jit(solution)/shard_map/while/body/eval_jaxpr/all_gather | solution.py:109
  1019.7 433.8 %all-gather.32.cloned.1.call-start = ((), (), s32[]{:S(2)}) async-start(), calls=%async_computation.24 | async-start | bytes 9437184 | tf_op jit(solution)/shard_map/while/body/eval_jaxpr/all_gather | solution.py:111
  1020.3 573.5 %reduce-scatter.25.cloned.1.call-start = ((), (), s32[]{:S(2)}) async-start(), calls=%async_computation.26 | async-start | bytes 10485760 | tf_op jit(solution)/shard_map/while/body/eval_jaxpr/reduce_scatter | solution.py:259
  1412.7 328.7 %reduce-scatter.23.cloned.1.call-start = ((), (), s32[]{:S(2)}) async-start(), calls=%async_computation.25 | async-start | bytes 10485760 | tf_op jit(solution)/shard_map/while/body/eval_jaxpr/reduce_scatter | solution.py:260
  1484.0 404.8 %reduce-scatter.27.cloned.1.call-start = ((), (), s32[]{:S(2)}) async-start(), calls=%async_computation.27 | async-start | bytes 10485760 | tf_op jit(solution)/shard_map/while/body/eval_jaxpr/reduce_scatter | solution.py:179
  1900.2 157.4 %reduce-scatter.19.cloned.1.call-start = ((), (), s32[]{:S(2)}) async-start(), calls=%async_computation.15 | async-start | bytes 221184
  1901.8 157.2 %reduce-scatter.21.cloned.1.call-start = ((), (), s32[]{:S(2)}) async-start(), calls=%async_computation.16 | async-start | bytes 294912
  1903.5 172.0 %reduce-scatter.13.cloned.1.call-start = ((), (), s32[]{:S(2)}) async-start(), calls=%async_computation.12 | async-start | bytes 2359296 | tf_op jit(solution)/shard_map/reduce_scatter | solution.py:290
  1907.4 232.8 %all-reduce.17.cloned.1.call-start = ((), (), s32[]{:S(2)}) async-start(), calls=%async_computation.17 | async-start | bytes 12582912
  1929.4 285.5 %reduce-scatter.15.cloned.1.call-start = ((), (), s32[]{:S(2)}) async-start(), calls=%async_computation.13 | async-start | bytes 9437184 | tf_op jit(solution)/shard_map/reduce_scatter | solution.py:293
  1938.6 351.4 %reduce-scatter.17.cloned.1.call-start = ((), (), s32[]{:S(2)}) async-start(), calls=%async_computation.14 | async-start | bytes 9437184 | tf_op jit(solution)/shard_map/reduce_scatter | solution.py:299
  (146 other events, 7771.3 us)
Sparse Core Ops, SparseCore 0:
  130.6 26.9 all-gather.23
  159.1 80.7 all-gather.25
  241.5 79.2 all-gather.21
  322.5 45.1 all-gather.19
  369.7 80.7 all-gather.27
  452.3 52.9 all-gather.29
  507.1 55.9 all-gather.31
  565.5 144.4 reduce-scatter.24
  712.3 145.1 reduce-scatter.22
  859.8 145.1 reduce-scatter.26
  1013.1 28.6 all-gather.23
  1043.2 80.7 all-gather.25
  1125.6 79.2 all-gather.21
  1206.7 45.1 all-gather.19
  1253.9 80.7 all-gather.27
  1336.4 52.9 all-gather.29
  1391.1 55.9 all-gather.31
  1449.3 144.4 reduce-scatter.24
  1596.2 145.1 reduce-scatter.22
  1743.6 145.1 reduce-scatter.26
Sparse Core Ops, SparseCore 1:
  1904.2 34.2 reduce-scatter.18
  1942.3 34.7 reduce-scatter.20
  1980.2 51.9 reduce-scatter.12
  2035.8 104.3 all-reduce.16
  2143.6 71.2 reduce-scatter.14
  2218.8 71.1 reduce-scatter.16
where the time goes:
time: 2310 us; the launch traced here: 2300 us
  waiting for transfers between devices  1340 us (58%)
  matrix products  387 us (17%)
  local copies, waits for them, and re-layouts  238 us (10%)
  blocking collectives  159 us (7%)
  other arithmetic  111 us (5%)
  loops' own time  25.3 us (1%)
    reduce_scatter x2, waiting for transfers between devices, micro_step(): lax.psum_scatter(grad_second, 'tensor', scatter_dimension=0, tiled=True)  295 us
    reduce_scatter x2, waiting for transfers between devices, micro_step(): lax.psum_scatter(attn_part + ffn_part, 'tensor', scatter_dimension=0, til...  286 us
    all_gather x2, waiting for transfers between devices, micro_step(): grad_full = lax.all_gather(rows_grad, 'tensor', axis=0, tiled=True)  165 us
    all_gather x2, waiting for transfers between devices, micro_step(): lax.all_gather(normed_one.astype(jnp.bfloat16), 'tensor', axis=0, tiled=T...  149 us
    unnamed x2, blocking collectives  123 us
    all_gather x2, waiting for transfers between devices, current_set(): lax.all_gather(shard_set[0], 'dp', axis=0, tiled=True)  93.9 us
    dynamic_update_slice x8, local copies, waits for them, and re-layouts, micro_step(): lax.scan(back_block, (zero_heads, zero_heads), (starts, lse_blocks))  92.7 us
    reduce_scatter x2, waiting for transfers between devices, micro_step(): lax.psum_scatter(grad_first, 'tensor', scatter_dimension=0, tiled=True)  79.3 us
  transfers between devices with their start and end apart: 30, of which 19 were waited for; matrix products, arithmetic and copies ran while one was open for 30% of the time, Pallas kernels for 0%

commit v1 on v0

--- a/solution.py
+++ b/solution.py
@@ -179,7 +179,16 @@
         branch = lax.psum_scatter(attn_part + ffn_part, "tensor", scatter_dimension=0, tiled=True)
         output_rows = (residual + branch + dense_shift + fc2_shift).astype(jnp.bfloat16)
         back_set = current_set()
-        grad_full = lax.all_gather(rows_grad, "tensor", axis=0, tiled=True)
+        ring = [rows_grad]
+        for hop in range(3):
+            ring.append(
+                lax.ppermute(ring[-1], "tensor", [(dev, (dev + 1) % 4) for dev in range(4)])
+            )
+        grad_full = jnp.roll(
+            jnp.concatenate(ring[::-1], axis=0),
+            (lax.axis_index("tensor") + 1) * ring[0].shape[0],
+            axis=0,
+        )
         grad_dense = jnp.einsum("lhe,ld->hed", mixed, grad_full, preferred_element_type=jnp.float32)
         grad_mixed = jnp.einsum(
             "ld,hed->lhe", grad_full, back_set[2], preferred_element_type=jnp.float32

time: 2310 us -> 2230 us (0.965)
  waiting for transfers between devices: 1340 us -> 1200 us
  starting transfers between devices: 18.6 us -> 45.9 us
  local copies, waits for them, and re-layouts: 238 us -> 262 us
    ppermute x0 -> x6, waiting for transfers between devices: none -> 214 us  [micro_step(): lax.ppermute(ring[-1], 'tensor', [(dev, (dev + 1) % 4) for dev in range(4)])]
    all_gather x2 -> x0, waiting for transfers between devices: 165 us -> none  [micro_step(): grad_full = lax.all_gather(rows_grad, 'tensor', axis=0, tiled=True)]
    all_gather x2, waiting for transfers between devices: 149 us -> 0.01 us  [micro_step(): lax.all_gather(normed_one.astype(jnp.bfloat16), 'tensor', axis=0, tiled=T...]
    ppermute x0 -> x6, starting transfers between devices: none -> 27.4 us  [micro_step(): lax.ppermute(ring[-1], 'tensor', [(dev, (dev + 1) % 4) for dev in range(4)])]
    all_gather x2, waiting for transfers between devices: 93.9 us -> 70.3 us  [current_set(): lax.all_gather(shard_set[0], 'dp', axis=0, tiled=True)]
  transfers between devices with their start and end apart: 30 -> 34, of which waited for: 19 -> 19; matrix products, arithmetic and copies ran while one was open for 30% -> 33% of each run, Pallas kernels for 0% -> 0%
where the time goes in v1:
time: 2230 us; the launch traced here: 2220 us
  waiting for transfers between devices  1200 us (54%)
  matrix products  395 us (18%)
  local copies, waits for them, and re-layouts  262 us (12%)
  blocking collectives  157 us (7%)
  other arithmetic  116 us (5%)
  starting transfers between devices  45.9 us (2%)
  loops' own time  24.8 us (1%)
    reduce_scatter x2, waiting for transfers between devices, micro_step(): lax.psum_scatter(grad_second, 'tensor', scatter_dimension=0, tiled=True)  295 us
    reduce_scatter x2, waiting for transfers between devices, micro_step(): lax.psum_scatter(attn_part + ffn_part, 'tensor', scatter_dimension=0, til...  286 us
    ppermute x6, waiting for transfers between devices, micro_step(): lax.ppermute(ring[-1], 'tensor', [(dev, (dev + 1) % 4) for dev in range(4)])  214 us
    unnamed x2, blocking collectives  123 us
    dynamic_update_slice x8, local copies, waits for them, and re-layouts, micro_step(): lax.scan(back_block, (zero_heads, zero_heads), (starts, lse_blocks))  93 us
    reduce_scatter x2, waiting for transfers between devices, micro_step(): lax.psum_scatter(grad_first, 'tensor', scatter_dimension=0, tiled=True)  75.4 us
    reduce_scatter x1, waiting for transfers between devices, per_device(): lax.psum_scatter(weight_totals[5].astype(jnp.bfloat16), 'dp', scatter_dim...  72.2 us
    reduce_scatter x1, waiting for transfers between devices, per_device(): lax.psum_scatter(weight_totals[3].astype(jnp.bfloat16), 'dp', scatter_dim...  72 us
  transfers between devices with their start and end apart: 34, of which 19 were waited for; matrix products, arithmetic and copies ran while one was open for 33% of the time, Pallas kernels for 0%

profile of v1, /device:TPU:0, one launch (start us, length us, event | category | flops | bytes accessed | tf_op | source)
XLA Modules:
  0.0 2217.5 jit_solution(5620455461615828725)
XLA Ops:
  58.2 58.6 %all-reduce.14 = (bf16[2048]{0:T(1024)(128)(2,1)S(1)}, bf16[2048]{0:T(1024)(128)(2,1)S(1)}, bf16[2048]{0:T(1024)(128)(2,1)S(1)}, bf16[2048]{0:T(1024)(128)(2,1)S...) all-reduce(bf16[2048]{0:T(1024)(128)(2,1)S(1)} %dynamic-update-slic, ...), channel_id=1, replica_groups=mesh['dp'=8,'tensor'=4] {'dp','tensor'}, use_global_device_ids=true, to_apply=%add | all-reduce | flops 12288 | bytes 49152
  127.6 1689.7 %while.108 = (s32[]{:T(128)}, f32[2048,2,768]{2,0,1:T(8,128)}, f32[2,768]{1,0:T(2,128)}, f32[2,256,2048]{2,1,0:T(8,128)}, f32[2048,2048]{1,0:T(8,128)}, /*index=...) while((s32[]{:T(128)}, f32[2048,2,768]{2,0,1:T(8,128)}, ...), condition=%wide.region_24.26_spmd.clone.clone.clone.clone, body=%wide.region_0.25_spmd.clone.clone.clone.clone.sunk | while | flops 81338195968 | bytes 852526464 | solution.py:289
  139.3 25.5 %collective-permute-done = bf16[256,2048]{1,0:T(8,128)(2,1)S(1)} collective-permute-done((bf16[256,2048]{1,0:T(8,128)(2,1)S(1)}, bf16[256,2048]{1,0:T(8,128)(2,1)S(1)}, u32[]{:S(2)}, u32[]{:S(2)}) %collective-permute-start) | collective-permute-done | bytes 1048608 | tf_op jit(solution)/shard_map/while/body/eval_jaxpr/ppermute | solution.py:185
  164.9 46.1 %collective-permute-done.1 = bf16[256,2048]{1,0:T(8,128)(2,1)} collective-permute-done((bf16[256,2048]{1,0:T(8,128)(2,1)S(1)}, bf16[256,2048]{1,0:T(8,128)(2,1)}, u32[]{:S(2)}, u32[]{:S(2)}) %collective-permute-start.1) | collective-permute-done | bytes 1048608 | tf_op jit(solution)/shard_map/while/body/eval_jaxpr/ppermute | solution.py:185
  230.6 40.7 %collective-permute-done.2 = bf16[256,2048]{1,0:T(8,128)(2,1)} collective-permute-done((bf16[256,2048]{1,0:T(8,128)(2,1)}, bf16[256,2048]{1,0:T(8,128)(2,1)}, u32[]{:S(2)}, u32[]{:S(2)}) %collective-permute-start.2) | collective-permute-done | bytes 1048608 | tf_op jit(solution)/shard_map/while/body/eval_jaxpr/ppermute | solution.py:185
  291.3 35.7 %all-gather.13.cloned.1.call-done = bf16[2048,2,768]{0,2,1:T(8,128)(2,1)} async-done(((bf16[256,2,768]{0,2,1:T(8,128)(2,1)}), bf16[2048,2,768]{0,2,1:T(8,128)(2,1)}) %all-gather.13.cloned.1.call-update) | async-done | bytes 6291472 | tf_op jit(solution)/shard_map/while/body/eval_jaxpr/all_gather | solution.py:106
  364.3 87.9 %while.110 = (s32[]{:T(128)}, f32[1024,2,256]{0,2,1:T(8,128)}, f32[1024,2,256]{0,2,1:T(8,128)}, f32[2,512,2,256]{1,0,3,2:T(2,128)}, s32[2]{0:T(128)S(1)}, /*inde...) while((s32[]{:T(128)}, f32[1024,2,256]{0,2,1:T(8,128)}, ...), condition=%wide.region_9.10_spmd.clone.clone, body=%wide.region_7.9_spmd.clone.clone.sunk | while | flops 2704015360 | bytes 111194568 | solution.py:250
  497.9 31.2 %fusion.255 = (bf16[1024,2048]{1,0:T(8,128)(2,1)}, f32[1024,2048]{1,0:T(8,128)}) fusion(f32[2048]{0:T(1024)S(1)} %bitcast.316, bf16[1024,2048]{1,0:T(8,128)(2,1)} %all-gather.19.cloned.1.call-done, bf16[2048,2048]{1,0:T(8,128)(2,1)} %all-gather.21.cloned.1.call-done), kind=kOutput, calls=%fused_computation.67.clone.1 | convolution fusion | flops 8728346624 | bytes 25174016 | tf_op jit(solution)/shard_map/while/body/eval_jaxpr/dot_general | solution.py:174
  626.3 42.8 %reduce-scatter.25.cloned.1.call-done = f32[256,2048]{1,0:T(8,128)} async-done(((f32[1024,2048]{1,0:T(8,128)}), f32[256,2048]{1,0:T(8,128)}) %reduce-scatter.25.cloned.1.call-update) | async-done | bytes 2097168 | tf_op jit(solution)/shard_map/while/body/eval_jaxpr/reduce_scatter | solution.py:268
  669.1 147.6 %reduce-scatter.23.cloned.1.call-done = f32[256,2048]{1,0:T(8,128)} async-done(((f32[1024,2048]{1,0:T(8,128)}), f32[256,2048]{1,0:T(8,128)}) %reduce-scatter.23.cloned.1.call-update) | async-done | bytes 2097168 | tf_op jit(solution)/shard_map/while/body/eval_jaxpr/reduce_scatter | solution.py:269
  821.1 143.1 %reduce-scatter.27.cloned.1.call-done = f32[256,2048]{1,0:T(8,128)} async-done(((f32[1024,2048]{1,0:T(8,128)}), f32[256,2048]{1,0:T(8,128)}) %reduce-scatter.27.cloned.1.call-update) | async-done | bytes 2097168 | tf_op jit(solution)/shard_map/while/body/eval_jaxpr/reduce_scatter | solution.py:179
  981.5 25.4 %collective-permute-done = bf16[256,2048]{1,0:T(8,128)(2,1)S(1)} collective-permute-done((bf16[256,2048]{1,0:T(8,128)(2,1)S(1)}, bf16[256,2048]{1,0:T(8,128)(2,1)S(1)}, u32[]{:S(2)}, u32[]{:S(2)}) %collective-permute-start) | collective-permute-done | bytes 1048608 | tf_op jit(solution)/shard_map/while/body/eval_jaxpr/ppermute | solution.py:185
  1006.9 45.7 %collective-permute-done.1 = bf16[256,2048]{1,0:T(8,128)(2,1)} collective-permute-done((bf16[256,2048]{1,0:T(8,128)(2,1)S(1)}, bf16[256,2048]{1,0:T(8,128)(2,1)}, u32[]{:S(2)}, u32[]{:S(2)}) %collective-permute-start.1) | collective-permute-done | bytes 1048608 | tf_op jit(solution)/shard_map/while/body/eval_jaxpr/ppermute | solution.py:185
  1083.8 30.9 %collective-permute-done.2 = bf16[256,2048]{1,0:T(8,128)(2,1)} collective-permute-done((bf16[256,2048]{1,0:T(8,128)(2,1)}, bf16[256,2048]{1,0:T(8,128)(2,1)}, u32[]{:S(2)}, u32[]{:S(2)}) %collective-permute-start.2) | collective-permute-done | bytes 1048608 | tf_op jit(solution)/shard_map/while/body/eval_jaxpr/ppermute | solution.py:185
  1134.9 34.6 %all-gather.13.cloned.1.call-done = bf16[2048,2,768]{0,2,1:T(8,128)(2,1)} async-done(((bf16[256,2,768]{0,2,1:T(8,128)(2,1)}), bf16[2048,2,768]{0,2,1:T(8,128)(2,1)}) %all-gather.13.cloned.1.call-update) | async-done | bytes 6291472 | tf_op jit(solution)/shard_map/while/body/eval_jaxpr/all_gather | solution.py:106
  1206.9 87.6 %while.110 = (s32[]{:T(128)}, f32[1024,2,256]{0,2,1:T(8,128)}, f32[1024,2,256]{0,2,1:T(8,128)}, f32[2,512,2,256]{1,0,3,2:T(2,128)}, s32[2]{0:T(128)S(1)}, /*inde...) while((s32[]{:T(128)}, f32[1024,2,256]{0,2,1:T(8,128)}, ...), condition=%wide.region_9.10_spmd.clone.clone, body=%wide.region_7.9_spmd.clone.clone.sunk | while | flops 2704015360 | bytes 111194568 | solution.py:250
  1340.4 31.4 %fusion.255 = (bf16[1024,2048]{1,0:T(8,128)(2,1)}, f32[1024,2048]{1,0:T(8,128)}) fusion(f32[2048]{0:T(1024)S(1)} %bitcast.316, bf16[1024,2048]{1,0:T(8,128)(2,1)} %all-gather.19.cloned.1.call-done, bf16[2048,2048]{1,0:T(8,128)(2,1)} %all-gather.21.cloned.1.call-done), kind=kOutput, calls=%fused_computation.67.clone.1 | convolution fusion | flops 8728346624 | bytes 25174016 | tf_op jit(solution)/shard_map/while/body/eval_jaxpr/dot_general | solution.py:174
  1479.0 32.6 %reduce-scatter.25.cloned.1.call-done = f32[256,2048]{1,0:T(8,128)} async-done(((f32[1024,2048]{1,0:T(8,128)}), f32[256,2048]{1,0:T(8,128)}) %reduce-scatter.25.cloned.1.call-update) | async-done | bytes 2097168 | tf_op jit(solution)/shard_map/while/body/eval_jaxpr/reduce_scatter | solution.py:268
  1511.6 147.4 %reduce-scatter.23.cloned.1.call-done = f32[256,2048]{1,0:T(8,128)} async-done(((f32[1024,2048]{1,0:T(8,128)}), f32[256,2048]{1,0:T(8,128)}) %reduce-scatter.23.cloned.1.call-update) | async-done | bytes 2097168 | tf_op jit(solution)/shard_map/while/body/eval_jaxpr/reduce_scatter | solution.py:269
  1663.5 143.0 %reduce-scatter.27.cloned.1.call-done = f32[256,2048]{1,0:T(8,128)} async-done(((f32[1024,2048]{1,0:T(8,128)}), f32[256,2048]{1,0:T(8,128)}) %reduce-scatter.27.cloned.1.call-update) | async-done | bytes 2097168 | tf_op jit(solution)/shard_map/while/body/eval_jaxpr/reduce_scatter | solution.py:179
  1907.2 64.1 %all-reduce.13 = (f32[2048]{0:T(1024)S(1)}, f32[2048]{0:T(1024)S(1)}, f32[2048]{0:T(1024)S(1)}, f32[2048]{0:T(1024)S(1)}, f32[2048]{0:T(1024)S(1)}, /*index=5*/f32[2048]{0:T(1024)S(1)}) all-reduce(f32[2048]{0:T(1024)S(1)} %copy-done.32, f32[2048]{0:T(1024)S(1)} %copy-done.35, ...), channel_id=5, replica_groups=mesh['dp'=8,'tensor'=4] {'dp','tensor'}, use_global_device_ids=true, to_apply=%region_26.28.clone | all-reduce | flops 12288 | bytes 98304
  1994.6 62.7 %all-reduce.17.cloned.1.call-done = bf16[2048,2,768]{2,1,0:T(2,128)(2,1)} async-done(((bf16[2048,2,768]{2,1,0:T(2,128)(2,1)}), bf16[2048,2,768]{2,1,0:T(2,128)(2,1)}) %all-reduce.17.cloned.1.call-update) | async-done | bytes 6291472
  2060.1 72.0 %reduce-scatter.15.cloned.1.call-done = bf16[256,2048]{1,0:T(8,128)(2,1)} async-done(((bf16[2048,2048]{1,0:T(8,128)(2,1)}), bf16[256,2048]{1,0:T(8,128)(2,1)}) %reduce-scatter.15.cloned.1.call-update) | async-done | bytes 1048592 | tf_op jit(solution)/shard_map/reduce_scatter | solution.py:302
  2134.8 72.2 %reduce-scatter.17.cloned.1.call-done = bf16[2048,256]{1,0:T(8,128)(2,1)} async-done(((bf16[2048,2048]{1,0:T(8,128)(2,1)}), bf16[2048,256]{1,0:T(8,128)(2,1)}) %reduce-scatter.17.cloned.1.call-update) | async-done | bytes 1048592 | tf_op jit(solution)/shard_map/reduce_scatter | solution.py:308
  (649 shorter events, 877.3 us)
Async XLA Ops:
  127.6 157.2 %all-gather.17.cloned.1.call-start = ((), (), s32[]{:S(2)}) async-start(), calls=%async_computation.20 | async-start | bytes 2359296 | tf_op jit(solution)/shard_map/while/body/eval_jaxpr/all_gather | solution.py:108
  128.3 163.0 %all-gather.15.cloned.1.call-start = ((), (), s32[]{:S(2)}) async-start(), calls=%async_computation.19 | async-start | bytes 5242880 | tf_op jit(solution)/shard_map/while/body/eval_jaxpr/all_gather | solution.py:141
  134.9 192.1 %all-gather.13.cloned.1.call-start = ((), (), s32[]{:S(2)}) async-start(), calls=%async_computation.18 | async-start | bytes 7077888 | tf_op jit(solution)/shard_map/while/body/eval_jaxpr/all_gather | solution.py:106
  135.6 362.3 %all-gather.19.cloned.1.call-start = ((), (), s32[]{:S(2)}) async-start(), calls=%async_computation.21 | async-start | bytes 5242880 | tf_op jit(solution)/shard_map/while/body/eval_jaxpr/all_gather | solution.py:142
  136.2 361.7 %all-gather.21.cloned.1.call-start = ((), (), s32[]{:S(2)}) async-start(), calls=%async_computation.22 | async-start | bytes 9437184 | tf_op jit(solution)/shard_map/while/body/eval_jaxpr/all_gather | solution.py:109
  136.8 392.3 %all-gather.23.cloned.1.call-start = ((), (), s32[]{:S(2)}) async-start(), calls=%async_computation.23 | async-start | bytes 9437184 | tf_op jit(solution)/shard_map/while/body/eval_jaxpr/all_gather | solution.py:111
  218.3 450.7 %reduce-scatter.25.cloned.1.call-start = ((), (), s32[]{:S(2)}) async-start(), calls=%async_computation.25 | async-start | bytes 10485760 | tf_op jit(solution)/shard_map/while/body/eval_jaxpr/reduce_scatter | solution.py:268
  488.7 328.0 %reduce-scatter.23.cloned.1.call-start = ((), (), s32[]{:S(2)}) async-start(), calls=%async_computation.24 | async-start | bytes 10485760 | tf_op jit(solution)/shard_map/while/body/eval_jaxpr/reduce_scatter | solution.py:269
  560.8 403.4 %reduce-scatter.27.cloned.1.call-start = ((), (), s32[]{:S(2)}) async-start(), calls=%async_computation.26 | async-start | bytes 10485760 | tf_op jit(solution)/shard_map/while/body/eval_jaxpr/reduce_scatter | solution.py:179
  969.3 158.9 %all-gather.17.cloned.1.call-start = ((), (), s32[]{:S(2)}) async-start(), calls=%async_computation.20 | async-start | bytes 2359296 | tf_op jit(solution)/shard_map/while/body/eval_jaxpr/all_gather | solution.py:108
  969.9 165.1 %all-gather.15.cloned.1.call-start = ((), (), s32[]{:S(2)}) async-start(), calls=%async_computation.19 | async-start | bytes 5242880 | tf_op jit(solution)/shard_map/while/body/eval_jaxpr/all_gather | solution.py:141
  976.4 193.2 %all-gather.13.cloned.1.call-start = ((), (), s32[]{:S(2)}) async-start(), calls=%async_computation.18 | async-start | bytes 7077888 | tf_op jit(solution)/shard_map/while/body/eval_jaxpr/all_gather | solution.py:106
  977.0 363.4 %all-gather.19.cloned.1.call-start = ((), (), s32[]{:S(2)}) async-start(), calls=%async_computation.21 | async-start | bytes 5242880 | tf_op jit(solution)/shard_map/while/body/eval_jaxpr/all_gather | solution.py:142
  977.7 362.6 %all-gather.21.cloned.1.call-start = ((), (), s32[]{:S(2)}) async-start(), calls=%async_computation.22 | async-start | bytes 9437184 | tf_op jit(solution)/shard_map/while/body/eval_jaxpr/all_gather | solution.py:109
  978.3 393.4 %all-gather.23.cloned.1.call-start = ((), (), s32[]{:S(2)}) async-start(), calls=%async_computation.23 | async-start | bytes 9437184 | tf_op jit(solution)/shard_map/while/body/eval_jaxpr/all_gather | solution.py:111
  1071.2 440.4 %reduce-scatter.25.cloned.1.call-start = ((), (), s32[]{:S(2)}) async-start(), calls=%async_computation.25 | async-start | bytes 10485760 | tf_op jit(solution)/shard_map/while/body/eval_jaxpr/reduce_scatter | solution.py:268
  1330.9 328.1 %reduce-scatter.23.cloned.1.call-start = ((), (), s32[]{:S(2)}) async-start(), calls=%async_computation.24 | async-start | bytes 10485760 | tf_op jit(solution)/shard_map/while/body/eval_jaxpr/reduce_scatter | solution.py:269
  1403.2 403.3 %reduce-scatter.27.cloned.1.call-start = ((), (), s32[]{:S(2)}) async-start(), calls=%async_computation.26 | async-start | bytes 10485760 | tf_op jit(solution)/shard_map/while/body/eval_jaxpr/reduce_scatter | solution.py:179
  1817.3 157.5 %reduce-scatter.19.cloned.1.call-start = ((), (), s32[]{:S(2)}) async-start(), calls=%async_computation.15 | async-start | bytes 221184
  1818.9 157.2 %reduce-scatter.21.cloned.1.call-start = ((), (), s32[]{:S(2)}) async-start(), calls=%async_computation.16 | async-start | bytes 294912
  1820.6 172.0 %reduce-scatter.13.cloned.1.call-start = ((), (), s32[]{:S(2)}) async-start(), calls=%async_computation.12 | async-start | bytes 2359296 | tf_op jit(solution)/shard_map/reduce_scatter | solution.py:299
  1824.5 232.8 %all-reduce.17.cloned.1.call-start = ((), (), s32[]{:S(2)}) async-start(), calls=%async_computation.17 | async-start | bytes 12582912
  1846.5 285.6 %reduce-scatter.15.cloned.1.call-start = ((), (), s32[]{:S(2)}) async-start(), calls=%async_computation.13 | async-start | bytes 9437184 | tf_op jit(solution)/shard_map/reduce_scatter | solution.py:302
  1855.7 351.4 %reduce-scatter.17.cloned.1.call-start = ((), (), s32[]{:S(2)}) async-start(), calls=%async_computation.14 | async-start | bytes 9437184 | tf_op jit(solution)/shard_map/reduce_scatter | solution.py:308
  (142 other events, 8666.4 us)
Sparse Core Ops, SparseCore 0:
  130.3 26.9 all-gather.16
  158.9 121.2 all-gather.14
  282.1 44.8 all-gather.12
  329.0 80.7 all-gather.18
  411.5 52.9 all-gather.20
  466.2 55.9 all-gather.22
  524.6 144.4 reduce-scatter.24
  671.4 145.1 reduce-scatter.22
  819.0 145.1 reduce-scatter.26
  971.7 28.6 all-gather.16
  1001.9 120.8 all-gather.14
  1124.6 44.9 all-gather.12
  1171.7 80.7 all-gather.18
  1254.2 52.9 all-gather.20
  1308.9 55.9 all-gather.22
  1367.1 144.4 reduce-scatter.24
  1513.8 145.1 reduce-scatter.22
  1661.3 145.1 reduce-scatter.26
Sparse Core Ops, SparseCore 1:
  1821.4 34.2 reduce-scatter.18
  1859.4 34.6 reduce-scatter.20
  1897.3 52.0 reduce-scatter.12
  1952.9 104.3 all-reduce.16
  2060.8 71.2 reduce-scatter.14
  2135.9 71.1 reduce-scatter.16
